TPU v7x, 512 devices: a whole 4x4x16 slice. The times are simulated.
512 devices in a mesh: band: 8 (over y, core), pw: 64 (over z, x).
Axes of the slice: x: 4, y: 4, z: 16, core: 2. Of those that a mesh axis runs over, the one named last changes fastest.
Arguments:
- occupied_bands: float32 [2, 16, 3328, 128], P(None, 'band', 'pw'), may hold values from -0.11742834 to 0.11742834
- iterate: float32 [2, 16, 3328, 128], P(None, 'band', 'pw'), may hold values from -2 to 2
- residual: float32 [2, 16, 3328, 128], P(None, 'band', 'pw'), may hold values from -25 to 25, as said below
- old_direction: float32 [2, 16, 3328, 128], P(None, 'band', 'pw'), may hold values from -25 to 25, as said below
- preconditioner: float32 [16, 3328, 128], P('band', 'pw'), may hold values from 0.1 to 1
- old_norm: float32 [16], P('band'), may hold values from 0.4 to 1.6
- eigenvalues: float32 [16], replicated, may hold values from -2 to -0.3
- band_slot: int32 [16], replicated, may hold values from 0 to 15, each once
- potential: float32 [128, 128, 128], P('pw'), may hold values from 0.2 to 1.5
- column_map: int32 [3328], replicated, may hold values from 0 to 16383, as said below
Outputs:
- new_iterate: float32 [2, 16, 3328, 128], P(None, 'band', 'pw')
- new_residual: float32 [2, 16, 3328, 128], P(None, 'band', 'pw')
- direction: float32 [2, 16, 3328, 128], P(None, 'band', 'pw')
- new_norm: float32 [16], P('band')
- density: float32 [128, 128, 128], P('pw', 'band')
Inputs may be any that keep to these rules, and one draw needn't show every extreme that they name: `residual`: random draw per entry, rough from column to column and frequency to frequency. `old_direction`: random draw per entry, rough from column to column and frequency to frequency. `column_map`: distinct flat indices; every column with signed a^2 + b^2 < 32^2 is present, the remaining columns lie outside that disc; the column of flat index 0 is present. `band_slot`: each global band index appears once.
All inputs are finite; a program needn't handle non-finite values.
Results may differ from a plain program's by a relative error of at most 0.0001.
Values sent between devices are 32-bit elements; how exact they have to be, the bound alone decides.
A program may use at most 64 MiB of HBM per device.

v0:
```python
import math
import jax
import jax.numpy as jnp
from jax import lax
from jax.sharding import PartitionSpec as P

exact_mode = lax.Precision.HIGHEST


def phase_table(grid_len, direction_sign):
    indices = jnp.arange(grid_len, dtype=jnp.int32)
    phases = indices[:, None] * indices[None, :] % grid_len
    angles = phases.astype(jnp.float32) * (2.0 * math.pi / grid_len)
    cosine = jnp.cos(angles)
    sine_part = jnp.sin(angles) * direction_sign
    return jnp.stack([jnp.stack([cosine, sine_part]), jnp.stack([-sine_part, cosine])])


def signed_index(values, grid_len):
    return jnp.where(values < grid_len // 2, values, values - grid_len)


def wave_squares(columns, grid_len):
    wave_x = signed_index(columns // grid_len, grid_len)
    wave_y = signed_index(columns % grid_len, grid_len)
    wave_z = signed_index(jnp.arange(grid_len, dtype=jnp.int32), grid_len)
    return (wave_x * wave_x + wave_y * wave_y)[:, None] + (wave_z * wave_z)[None, :]


def correlation(band_rows, vectors):
    real_part = jnp.einsum("pvck,pnck->vn", band_rows, vectors, precision=exact_mode)
    imag_part = jnp.einsum(
        "vck,nck->vn", band_rows[0], vectors[1], precision=exact_mode
    ) - jnp.einsum("vck,nck->vn", band_rows[1], vectors[0], precision=exact_mode)
    return jnp.stack([real_part, imag_part])


def expand(band_rows, weights):
    real_part = jnp.einsum(
        "vck,vn->nck", band_rows[0], weights[0], precision=exact_mode
    ) - jnp.einsum("vck,vn->nck", band_rows[1], weights[1], precision=exact_mode)
    imag_part = jnp.einsum(
        "vck,vn->nck", band_rows[0], weights[1], precision=exact_mode
    ) + jnp.einsum("vck,vn->nck", band_rows[1], weights[0], precision=exact_mode)
    return jnp.stack([real_part, imag_part])


def column_transform(coefficients, phase_grid):
    mixed_cols = jnp.einsum("pbck,pqkz->qbzc", coefficients, phase_grid, precision=exact_mode)
    return lax.all_to_all(mixed_cols, "pw", split_axis=2, concat_axis=3, tiled=True)


def to_grid(columns, inverse_map, phase_grid, grid_len):
    item_rows = columns.shape[1]
    col_count = columns.shape[2]
    rows_first = columns.reshape(2 * item_rows, col_count).T
    padded = jnp.concatenate([rows_first, jnp.zeros((1, 2 * item_rows), jnp.float32)], axis=0)
    placed = jnp.take(padded, inverse_map, axis=0)
    field_grid = placed.T.reshape(2, item_rows, grid_len, grid_len)
    field_grid = jnp.einsum("pzxk,pqky->qzxy", field_grid, phase_grid, precision=exact_mode)
    return jnp.einsum("pzky,pqkx->qzxy", field_grid, phase_grid, precision=exact_mode)


def from_grid(field_grid, column_map, phase_grid, grid_len):
    item_rows = field_grid.shape[1]
    field_grid = jnp.einsum("pzxk,pqky->qzxy", field_grid, phase_grid, precision=exact_mode)
    field_grid = jnp.einsum("pzky,pqkx->qzxy", field_grid, phase_grid, precision=exact_mode)
    cells_first = field_grid.reshape(2 * item_rows, grid_len * grid_len).T
    picked = jnp.take(cells_first, column_map, axis=0)
    return picked.T.reshape(2, item_rows, column_map.shape[0])


def on_device(
    occupied_bands,
    iterate,
    residual,
    old_direction,
    preconditioner,
    old_norm,
    eigenvalues,
    band_slot,
    potential,
    column_map,
):
    grid_len = potential.shape[1]
    planes = potential.shape[0]
    local_bands = iterate.shape[1]
    local_cols = iterate.shape[2]
    col_count = column_map.shape[0]
    total_pw = col_count * grid_len
    forward_table = phase_table(grid_len, 1.0)
    inverse_table = phase_table(grid_len, -1.0)
    inverse_map = (
        jnp.full((grid_len * grid_len,), col_count, jnp.int32)
        .at[column_map]
        .set(jnp.arange(col_count, dtype=jnp.int32))
    )
    my_columns = lax.dynamic_slice_in_dim(column_map, lax.axis_index("pw") * local_cols, local_cols)
    squares = wave_squares(my_columns, grid_len)
    kinetic = squares.astype(jnp.float32) * (4.0 / (grid_len * grid_len))
    sphere = (squares < grid_len // 4 * (grid_len // 4)).astype(jnp.float32)
    occupied = occupied_bands * sphere
    start_wave = iterate * sphere
    masked_residual = residual * sphere
    previous = old_direction * sphere
    weight = preconditioner * sphere
    owner_ids = lax.dynamic_slice_in_dim(
        band_slot, lax.axis_index("band") * local_bands, local_bands
    )
    select = (
        owner_ids[:, None] == jnp.arange(band_slot.shape[0], dtype=jnp.int32)[None, :]
    ).astype(jnp.float32)
    band_energy = jnp.dot(select, eigenvalues, precision=exact_mode)
    all_occupied = lax.all_gather(occupied_bands, "band", axis=1, tiled=True) * sphere
    smoothed = weight[None] * masked_residual
    norm_local = (
        jnp.sum(weight[None] * masked_residual * masked_residual, axis=(0, 2, 3)) / total_pw
    )
    new_norm = lax.psum(norm_local, "pw")
    beta_ratio = new_norm / old_norm
    direction = smoothed + beta_ratio[None, :, None, None] * previous
    weights = lax.psum(correlation(all_occupied, direction), "pw")
    projected = expand(all_occupied, weights)
    direction_cols = column_transform(direction, forward_table)
    field_grid = to_grid(
        direction_cols.reshape(2, local_bands * planes, -1), inverse_map, forward_table, grid_len
    )
    field_grid = (
        field_grid.reshape(2, local_bands, planes, grid_len, grid_len) * potential[None, None]
    ).reshape(2, local_bands * planes, grid_len, grid_len)
    returned = from_grid(field_grid, column_map, inverse_table, grid_len)
    gathered_back = lax.all_to_all(
        returned.reshape(2, local_bands, planes, -1), "pw", split_axis=3, concat_axis=2, tiled=True
    )
    local_potential = jnp.einsum(
        "pbzc,pqzk->qbck", gathered_back, inverse_table, precision=exact_mode
    ) / float(grid_len**3)
    applied = (
        local_potential * sphere
        + (kinetic[None, None] - band_energy[None, :, None, None]) * direction
        + projected
    )
    curvature_local = jnp.sum(direction * applied, axis=(0, 2, 3)) / total_pw
    curvature = lax.psum(curvature_local, "pw")
    step_size = new_norm / curvature
    new_iterate = start_wave + step_size[None, :, None, None] * direction
    new_residual = masked_residual - step_size[None, :, None, None] * applied
    joined = column_transform(jnp.concatenate([occupied, new_iterate], axis=1), forward_table)
    both_grids = to_grid(
        joined.reshape(2, 2 * local_bands * planes, -1), inverse_map, forward_table, grid_len
    )
    both_grids = both_grids.reshape(2, 2, local_bands, planes, grid_len, grid_len)
    density_local = jnp.sum(both_grids[:, 0] * both_grids[:, 1], axis=(0, 1)) * (4.0 / total_pw)
    density = lax.psum_scatter(density_local, "band", scatter_dimension=1, tiled=True)
    return (new_iterate, new_residual, direction, new_norm, density)


def solution(mesh):
    in_specs = (
        P(None, "band", "pw", None),
        P(None, "band", "pw", None),
        P(None, "band", "pw", None),
        P(None, "band", "pw", None),
        P("band", "pw", None),
        P("band"),
        P(),
        P(),
        P("pw", None, None),
        P(),
    )
    out_specs = (
        P(None, "band", "pw", None),
        P(None, "band", "pw", None),
        P(None, "band", "pw", None),
        P("band"),
        P("pw", "band", None),
    )
    return jax.shard_map(
        on_device, mesh=mesh, in_specs=in_specs, out_specs=out_specs, check_vma=False
    )
```

profile of v0, /device:TPU:4, one launch (start us, length us, event | category | flops | bytes accessed | tf_op | source)
XLA Modules:
  0.0 811.0 jit_solution(9233818517082111334)
XLA Ops:
  11.4 145.6 %psum.21 = f32[2]{0:T(128)S(1)} all-reduce(f32[2]{0:T(128)S(1)} %broadcast_multiply_fusion.4), channel_id=1, replica_groups=mesh['band'=8,'pw'=64] {'pw'}, use_global_device_ids=true, to_apply=%region_1.2 | all-reduce | flops 2 | bytes 16 | tf_op jit(solution)/shard_map/psum | solution.py:119
  161.9 11.0 %all-to-all-start = ((f32[64,1,416]{2,1,0:T(1,128)}), f32[64,1,416]{2,1,0:T(1,128)S(1)}, u32[]{:S(2)}, u32[]{:S(2)}) async-start(f32[64,1,416]{2,1,0:T(1,128)} %reshape.312), calls=%async_computation | async-start | bytes 262144 | tf_op jit(solution)/shard_map/all_to_all | solution.py:50
  175.2 14.0 %all_gather.3 = f32[2,16,52,128]{3,0,2,1:T(2,128)S(1)} all-gather(f32[2,2,52,128]{3,0,2,1:T(2,128)S(1)} %copy.102), channel_id=1, replica_groups=mesh['band'=8,'pw'=64] {'band'}, dimensions={1}, use_global_device_ids=true | all-gather | bytes 958464 | tf_op jit(solution)/shard_map/all_gather | solution.py:114
  191.8 138.8 %psum.22 = f32[2,16,2]{1,2,0:T(2,128)S(1)} all-reduce(f32[2,16,2]{1,2,0:T(2,128)S(1)} %pad_maximum_fusion.12), channel_id=1, replica_groups=mesh['band'=8,'pw'=64] {'pw'}, use_global_device_ids=true, to_apply=%region_3.4 | all-reduce | flops 64 | bytes 512 | tf_op jit(solution)/shard_map/psum | solution.py:122
  335.8 12.7 %scatter_custom_fusion = s32[16384]{0:T(1024)S(1)} fusion(s32[3328]{0:T(1024)S(1)} %compare_select_fusion.1, s32[3328]{0:T(1024)S(1)} %iota.54, s32[]{:T(128)} %constant.107.clone.1), kind=kCustom, calls=%fused_computation.104 | custom fusion | bytes 65540 | tf_op jit(solution)/shard_map/scatter | solution.py:96
  353.0 60.2 %gather_fusion = f32[16384,8]{1,0:T(8,128)} fusion(f32[3329,8]{1,0:T(8,128)S(1)} %concatenate.9, s32[16384]{0:T(1024)} %fusion.49), kind=kCustom, calls=%fused_computation | custom fusion | bytes 1114112 | tf_op jit(solution)/shard_map/jit(_take)/gather | solution.py:58
  413.2 13.1 %select_bitcast_fusion.1 = f32[8,16384]{0,1:T(8,128)} fusion(f32[16384,8]{1,0:T(8,128)} %gather_fusion, pred[16384]{0:T(1024)(128)(4,1)S(1)} %copy-done.24), kind=kLoop, calls=%fused_computation.5 | loop fusion | flops 131072 | bytes 1064960 | tf_op jit(solution)/shard_map/jit(_take)/select_n | solution.py:58
  426.3 5.6 copy.86
  436.8 5.3 copy.95
  442.0 8.8 %gather_fusion.1 = f32[3328,8]{1,0:T(8,128)S(1)} fusion(f32[16384,8]{1,0:T(8,128)} %bitcast.224, s32[4096]{0:T(1024)S(1)} %copy-done.30), kind=kCustom, calls=%fused_computation.1 | custom fusion | bytes 226304 | tf_op jit(solution)/shard_map/jit(_take)/gather | solution.py:69
  452.7 6.6 reshape.309
  459.3 10.1 %reshape.314 = f32[64,1,416]{2,1,0:T(1,128)} reshape(f32[3328,2,2,2]{3,2,1,0:T(2,128)} %bitcast.226) | data formatting | bytes 212992
  469.4 14.6 %all-to-all-start.1 = ((f32[64,1,416]{2,1,0:T(1,128)}), f32[64,1,416]{2,1,0:T(1,128)S(1)}, u32[]{:S(2)}, u32[]{:S(2)}) async-start(f32[64,1,416]{2,1,0:T(1,128)} %reshape.314), calls=%async_computation.1 | async-start | bytes 262144 | tf_op jit(solution)/shard_map/all_to_all | solution.py:132
  484.3 14.1 %all-to-all-done.1 = f32[64,1,416]{2,1,0:T(1,128)S(1)} async-done(((f32[64,1,416]{2,1,0:T(1,128)}), f32[64,1,416]{2,1,0:T(1,128)S(1)}, u32[]{:S(2)}, u32[]{:S(2)}) %all-to-all-start.1) | async-done | bytes 106528 | tf_op jit(solution)/shard_map/all_to_all | solution.py:132
  499.4 11.8 %reshape.315 = f32[3328,2,2,2]{3,2,1,0:T(2,128)} reshape(f32[64,416]{1,0:T(8,128)S(1)} %reduce.2) | data formatting | bytes 212992
  511.2 10.3 %copy.165 = f32[2,2,2,64,52]{4,3,2,1,0:T(8,128)S(1)} copy(f32[2,2,2,64,52]{2,1,0,4,3:T(2,128)} %bitcast.225) | data formatting | bytes 212992 | tf_op jit(solution)/shard_map/all_to_all | solution.py:132
  522.4 136.6 %psum.23 = f32[2]{0:T(128)S(1)} all-reduce(f32[2]{0:T(128)S(1)} %broadcast_multiply_fusion.3), channel_id=1, replica_groups=mesh['band'=8,'pw'=64] {'pw'}, use_global_device_ids=true, to_apply=%region_5.6 | all-reduce | flops 2 | bytes 16 | tf_op jit(solution)/shard_map/psum | solution.py:144
  662.0 26.3 %all_to_all.48 = f32[64,1,832]{2,1,0:T(1,128)S(1)} all-to-all(f32[64,1,832]{2,1,0:T(1,128)S(1)} %reshape.316), channel_id=1, replica_groups=mesh['band'=8,'pw'=64] {'pw'}, dimensions={0} | all-to-all | bytes 425984 | tf_op jit(solution)/shard_map/all_to_all | solution.py:50
  691.5 60.0 %gather_fusion.2 = f32[16384,16]{1,0:T(8,128)} fusion(f32[3329,16]{1,0:T(8,128)S(1)} %concatenate.11, s32[16384]{0:T(1024)} %fusion.49), kind=kCustom, calls=%fused_computation.2 | custom fusion | bytes 2162688 | tf_op jit(solution)/shard_map/jit(_take)/gather | solution.py:58
  751.5 13.2 %select_bitcast_fusion = f32[16,16384]{0,1:T(8,128)} fusion(f32[16384,16]{1,0:T(8,128)} %gather_fusion.2, pred[16384]{0:T(1024)(128)(4,1)S(1)} %copy-done.25), kind=kLoop, calls=%fused_computation.4 | loop fusion | flops 262144 | bytes 2113536 | tf_op jit(solution)/shard_map/jit(_take)/select_n | solution.py:58
  764.7 5.2 copy.118
  769.8 2.0 convolution_bitcast_fusion
  771.8 1.9 fusion.20
  776.6 27.5 %reduce-scatter.2.cloned.1.call-done = f32[2,16,128]{2,1,0:T(8,128)} async-done(((f32[2,128,128]{2,1,0:T(8,128)}), f32[2,16,128]{2,1,0:T(8,128)}) %reduce-scatter.2.cloned.1.call-update) | async-done | bytes 16400 | tf_op jit(solution)/shard_map/reduce_scatter | solution.py:154
  (146 shorter events, 41.0 us)
Async XLA Ops:
  7.2 342.1 %copy-start = (f32[16]{0:T(128)S(1)}, f32[16]{0:T(128)}, u32[]{:S(2)}) copy-start(f32[16]{0:T(128)} %param.16) | copy-start | bytes 196
  7.2 342.0 %copy-start.31 = (s32[16]{0:T(128)S(1)}, s32[16]{0:T(128)}, u32[]{:S(2)}) copy-start(s32[16]{0:T(128)} %param.17) | copy-start | bytes 196
  8.6 343.6 %copy-start.13 = (f32[52,128]{1,0:T(8,128)}, f32[52,128]{1,0:T(8,128)S(1)}, u32[]{:S(2)}) copy-start(f32[52,128]{1,0:T(8,128)S(1)} %fusion.58) | copy-start | bytes 79876
  158.7 194.2 %copy-start.6 = (f32[2,2,52,128]{3,2,1,0:T(8,128)}, f32[2,2,52,128]{3,2,1,0:T(8,128)S(1)}, u32[]{:S(2)}) copy-start(f32[2,2,52,128]{3,2,1,0:T(8,128)S(1)} %multiply_add_fusion) | copy-start | bytes 319492
  161.9 188.2 %all-to-all-start = ((f32[64,1,416]{2,1,0:T(1,128)}), f32[64,1,416]{2,1,0:T(1,128)S(1)}, u32[]{:S(2)}, u32[]{:S(2)}) async-start(f32[64,1,416]{2,1,0:T(1,128)} %reshape.312), calls=%async_computation | async-start | bytes 262144 | tf_op jit(solution)/shard_map/all_to_all | solution.py:50
  353.0 60.2 %copy-start.24 = (pred[16384]{0:T(1024)(128)(4,1)S(1)}, pred[16384]{0:T(1024)(128)(4,1)}, u32[]{:S(2)}) copy-start(pred[16384]{0:T(1024)(128)(4,1)} %compare_and_fusion) | copy-start | bytes 49156
  452.6 31.6 %copy-start.20 = (f32[2,52,128]{2,0,1:T(2,128)S(1)}, f32[2,52,128]{2,0,1:T(2,128)}, u32[]{:S(2)}) copy-start(f32[2,52,128]{2,0,1:T(2,128)} %fusion.15) | copy-start | bytes 159748
  452.6 31.6 %copy-start.21 = (f32[2,52,128]{2,0,1:T(2,128)S(1)}, f32[2,52,128]{2,0,1:T(2,128)}, u32[]{:S(2)}) copy-start(f32[2,52,128]{2,0,1:T(2,128)} %fusion.17) | copy-start | bytes 159748
  452.6 31.5 %copy-start.22 = (f32[2,52,128]{2,0,1:T(2,128)S(1)}, f32[2,52,128]{2,0,1:T(2,128)}, u32[]{:S(2)}) copy-start(f32[2,52,128]{2,0,1:T(2,128)} %fusion.14) | copy-start | bytes 159748
  452.7 31.5 %copy-start.23 = (f32[2,52,128]{2,0,1:T(2,128)S(1)}, f32[2,52,128]{2,0,1:T(2,128)}, u32[]{:S(2)}) copy-start(f32[2,52,128]{2,0,1:T(2,128)} %fusion.16) | copy-start | bytes 159748
  469.4 52.3 %copy-start.7 = (f32[2,2,52,128]{3,2,1,0:T(8,128)S(1)}, f32[2,2,52,128]{3,2,1,0:T(8,128)}, u32[]{:S(2)}) copy-start(f32[2,2,52,128]{3,2,1,0:T(8,128)} %copy-done.6) | copy-start | bytes 319492
  469.4 52.3 %copy-start.10 = (f32[1,2,128,128]{3,2,1,0:T(8,128)S(1)}, f32[1,2,128,128]{3,2,1,0:T(8,128)}, u32[]{:S(2)}) copy-start(f32[1,2,128,128]{3,2,1,0:T(8,128)} %get-tuple-element.22) | copy-start | bytes 393220
  469.4 52.3 %copy-start.12 = (f32[1,2,128,128]{3,2,1,0:T(8,128)S(1)}, f32[1,2,128,128]{3,2,1,0:T(8,128)}, u32[]{:S(2)}) copy-start(f32[1,2,128,128]{3,2,1,0:T(8,128)} %get-tuple-element.25) | copy-start | bytes 393220
  469.4 52.3 %copy-start.27 = (f32[52,128]{1,0:T(8,128)S(1)}, f32[52,128]{1,0:T(8,128)}, u32[]{:S(2)}) copy-start(f32[52,128]{1,0:T(8,128)} %get-tuple-element.30) | copy-start | bytes 79876
  469.4 189.7 %copy-start.33 = (f32[2]{0:T(128)S(1)}, f32[2]{0:T(128)}, u32[]{:S(2)}) copy-start(f32[2]{0:T(128)} %copy-done.32) | copy-start | bytes 28
  469.4 189.6 %copy-start.14 = (f32[52,128]{1,0:T(8,128)S(1)}, f32[52,128]{1,0:T(8,128)}, u32[]{:S(2)}) copy-start(f32[52,128]{1,0:T(8,128)} %copy-done.13) | copy-start | bytes 79876
  469.4 189.6 %copy-start.17 = (f32[2,2,52,128]{3,1,2,0:T(2,128)S(1)}, f32[2,2,52,128]{3,1,2,0:T(2,128)}, u32[]{:S(2)}) copy-start(f32[2,2,52,128]{3,1,2,0:T(2,128)} %param.12) | copy-start | bytes 319492
  469.4 189.6 %copy-start.29 = (f32[2,2,52,128]{3,1,2,0:T(2,128)S(1)}, f32[2,2,52,128]{3,1,2,0:T(2,128)}, u32[]{:S(2)}) copy-start(f32[2,2,52,128]{3,1,2,0:T(2,128)} %param.11) | copy-start | bytes 319492
  469.4 29.0 %all-to-all-start.1 = ((f32[64,1,416]{2,1,0:T(1,128)}), f32[64,1,416]{2,1,0:T(1,128)S(1)}, u32[]{:S(2)}, u32[]{:S(2)}) async-start(f32[64,1,416]{2,1,0:T(1,128)} %reshape.314), calls=%async_computation.1 | async-start | bytes 262144 | tf_op jit(solution)/shard_map/all_to_all | solution.py:132
  484.0 320.1 %reduce-scatter.2.cloned.1.call-start = ((), (), s32[]{:S(2)}) async-start(), calls=%async_computation.4 | async-start | bytes 147456 | tf_op jit(solution)/shard_map/reduce_scatter | solution.py:154
  484.2 176.2 %copy-start.4 = (f32[1,2,128,128]{3,2,0,1:T(8,128)S(1)}, f32[1,2,128,128]{3,2,0,1:T(8,128)}, u32[]{:S(2)}) copy-start(f32[1,2,128,128]{3,2,0,1:T(8,128)} %copy-done.2) | copy-start | bytes 393220
  484.2 176.2 %copy-start.19 = (f32[2,2,52,128]{3,2,1,0:T(8,128)S(1)}, f32[2,2,52,128]{3,2,1,0:T(8,128)}, u32[]{:S(2)}) copy-start(f32[2,2,52,128]{3,2,1,0:T(8,128)} %get-tuple-element.28) | copy-start | bytes 319492
  691.5 60.0 %copy-start.25 = (pred[16384]{0:T(1024)(128)(4,1)S(1)}, pred[16384]{0:T(1024)(128)(4,1)}, u32[]{:S(2)}) copy-start(pred[16384]{0:T(1024)(128)(4,1)} %compare_and_fusion) | copy-start | bytes 49156
  751.5 52.6 %copy-start.1 = (f32[16]{0:T(128)S(1)}, f32[16]{0:T(128)}, u32[]{:S(2)}) copy-start(f32[16]{0:T(128)} %param.16) | copy-start | bytes 196
  (13 other events, 113.0 us)
Sparse Core Ops, SparseCore 0:
  774.6 29.4 reduce-scatter.1
where the time goes:
time: 815 us; the launch traced here: 811 us
  blocking collectives  461 us (57%)
  local copies, waits for them, and re-layouts  208 us (26%)
  other arithmetic  43.7 us (5%)
  waiting for transfers between devices  41.7 us (5%)
  starting transfers between devices  25.6 us (3%)
  matrix products  15.8 us (2%)
  between operations  14.7 us (2%)
    psum x1, blocking collectives, on_device(): new_norm = lax.psum(norm_local, 'pw')  146 us
    psum x1, blocking collectives, on_device(): weights = lax.psum(correlation(all_occupied, direction), 'pw')  139 us
    psum x1, blocking collectives, on_device(): curvature = lax.psum(curvature_local, 'pw')  137 us
    gather x2, local copies, waits for them, and re-layouts, to_grid(): placed = jnp.take(padded, inverse_map, axis=0)  120 us
    unnamed x80, local copies, waits for them, and re-layouts  30.2 us
    reduce_scatter x1, waiting for transfers between devices, on_device(): lax.psum_scatter(density_local, 'band', scatter_dimension=1, tiled=True)  27.5 us
    all_to_all x1, blocking collectives, column_transform(): lax.all_to_all(mixed_cols, 'pw', split_axis=2, concat_axis=3, tiled=True)  26.3 us
    select_n x2, other arithmetic, to_grid(): placed = jnp.take(padded, inverse_map, axis=0)  26.3 us
  transfers between devices with their start and end apart: 3, of which 2 were waited for; matrix products, arithmetic and copies ran while one was open for 3% of the time, Pallas kernels for 0%

commit v1 on v0

--- a/solution.py
+++ b/solution.py
@@ -1,10 +1,19 @@
+import functools
 import math
 import jax
 import jax.numpy as jnp
 from jax import lax
 from jax.sharding import PartitionSpec as P
+from jax.lax import all_gather
 
 exact_mode = lax.Precision.HIGHEST
+
+
+def process_leaf(sample, group_axis):
+    return jnp.sum(all_gather(sample, group_axis), axis=0)
+
+
+proceed_slots = functools.partial(process_leaf, group_axis="pw")
 
 
 def phase_table(grid_len, direction_sign):
@@ -119,7 +128,7 @@
     new_norm = lax.psum(norm_local, "pw")
     beta_ratio = new_norm / old_norm
     direction = smoothed + beta_ratio[None, :, None, None] * previous
-    weights = lax.psum(correlation(all_occupied, direction), "pw")
+    weights = proceed_slots(correlation(all_occupied, direction))
     projected = expand(all_occupied, weights)
     direction_cols = column_transform(direction, forward_table)
     field_grid = to_grid(

time: 815 us -> 782 us (0.960)
  the two profiles are of different devices: /device:TPU:4 before, /device:TPU:2 now
where the time goes in v1:
time: 782 us; the launch traced here: 772 us
  blocking collectives  423 us (54%)
  local copies, waits for them, and re-layouts  208 us (27%)
  other arithmetic  43.7 us (6%)
  waiting for transfers between devices  42.1 us (5%)
  starting transfers between devices  23.9 us (3%)
  matrix products  15.8 us (2%)
  between operations  14.9 us (2%)
    psum x1, blocking collectives, on_device(): new_norm = lax.psum(norm_local, 'pw')  146 us
    psum x1, blocking collectives, on_device(): curvature = lax.psum(curvature_local, 'pw')  141 us
    gather x2, local copies, waits for them, and re-layouts, to_grid(): placed = jnp.take(padded, inverse_map, axis=0)  120 us
    all_gather x1, blocking collectives, process_leaf(): return jnp.sum(all_gather(sample, group_axis), axis=0)  99.9 us
    unnamed x80, local copies, waits for them, and re-layouts  30.2 us
    reduce_scatter x1, waiting for transfers between devices, on_device(): lax.psum_scatter(density_local, 'band', scatter_dimension=1, tiled=True)  27.2 us
    select_n x2, other arithmetic, to_grid(): placed = jnp.take(padded, inverse_map, axis=0)  26.3 us
    all_to_all x1, blocking collectives, column_transform(): lax.all_to_all(mixed_cols, 'pw', split_axis=2, concat_axis=3, tiled=True)  22.6 us
  transfers between devices with their start and end apart: 3, of which 2 were waited for; matrix products, arithmetic and copies ran while one was open for 3% of the time, Pallas kernels for 0%

profile of v1, /device:TPU:2, one launch (start us, length us, event | category | flops | bytes accessed | tf_op | source)
XLA Modules:
  0.0 771.8 jit_solution(13776496611948767670)
XLA Ops:
  11.4 145.7 %psum.14 = f32[2]{0:T(128)S(1)} all-reduce(f32[2]{0:T(128)S(1)} %broadcast_multiply_fusion.4), channel_id=1, replica_groups=mesh['band'=8,'pw'=64] {'pw'}, use_global_device_ids=true, to_apply=%region_1.2 | all-reduce | flops 2 | bytes 16 | tf_op jit(solution)/shard_map/psum | solution.py:128
  162.0 10.9 %all-to-all-start = ((f32[64,1,416]{2,1,0:T(1,128)}), f32[64,1,416]{2,1,0:T(1,128)S(1)}, u32[]{:S(2)}, u32[]{:S(2)}) async-start(f32[64,1,416]{2,1,0:T(1,128)} %reshape.313), calls=%async_computation | async-start | bytes 262144 | tf_op jit(solution)/shard_map/all_to_all | solution.py:59
  175.3 14.0 %all_gather.9 = f32[2,16,52,128]{3,0,2,1:T(2,128)S(1)} all-gather(f32[2,2,52,128]{3,0,2,1:T(2,128)S(1)} %copy.102), channel_id=1, replica_groups=mesh['band'=8,'pw'=64] {'band'}, dimensions={1}, use_global_device_ids=true | all-gather | bytes 958464 | tf_op jit(solution)/shard_map/all_gather | solution.py:123
  191.8 99.9 %all-gather = f32[128,16,2]{1,2,0:T(2,128)S(1)} all-gather(f32[2,16,2]{1,2,0:T(2,128)S(1)} %pad_maximum_fusion.12), channel_id=2, replica_groups=mesh['band'=8,'pw'=64] {'pw'}, dimensions={0}, use_global_device_ids=true | all-gather | bytes 16640 | tf_op jit(solution)/shard_map/all_gather | solution.py:13
  296.9 12.7 %scatter_custom_fusion = s32[16384]{0:T(1024)S(1)} fusion(s32[3328]{0:T(1024)S(1)} %compare_select_fusion.1, s32[3328]{0:T(1024)S(1)} %iota.54, s32[]{:T(128)} %constant.107.clone.1), kind=kCustom, calls=%fused_computation.104 | custom fusion | bytes 65540 | tf_op jit(solution)/shard_map/scatter | solution.py:105
  314.2 60.4 %gather_fusion = f32[16384,8]{1,0:T(8,128)} fusion(f32[3329,8]{1,0:T(8,128)S(1)} %concatenate.9, s32[16384]{0:T(1024)} %fusion.49), kind=kCustom, calls=%fused_computation | custom fusion | bytes 1114112 | tf_op jit(solution)/shard_map/jit(_take)/gather | solution.py:67
  374.6 13.1 %select_bitcast_fusion.1 = f32[8,16384]{0,1:T(8,128)} fusion(f32[16384,8]{1,0:T(8,128)} %gather_fusion, pred[16384]{0:T(1024)(128)(4,1)S(1)} %copy-done.24), kind=kLoop, calls=%fused_computation.5 | loop fusion | flops 131072 | bytes 1064960 | tf_op jit(solution)/shard_map/jit(_take)/select_n | solution.py:67
  387.8 5.6 copy.86
  398.2 5.3 copy.95
  403.5 8.8 %gather_fusion.1 = f32[3328,8]{1,0:T(8,128)S(1)} fusion(f32[16384,8]{1,0:T(8,128)} %bitcast.225, s32[4096]{0:T(1024)S(1)} %copy-done.30), kind=kCustom, calls=%fused_computation.1 | custom fusion | bytes 226304 | tf_op jit(solution)/shard_map/jit(_take)/gather | solution.py:78
  414.1 6.6 reshape.310
  420.7 10.1 %reshape.315 = f32[64,1,416]{2,1,0:T(1,128)} reshape(f32[3328,2,2,2]{3,2,1,0:T(2,128)} %bitcast.227) | data formatting | bytes 212992
  430.9 12.9 %all-to-all-start.1 = ((f32[64,1,416]{2,1,0:T(1,128)}), f32[64,1,416]{2,1,0:T(1,128)S(1)}, u32[]{:S(2)}, u32[]{:S(2)}) async-start(f32[64,1,416]{2,1,0:T(1,128)} %reshape.315), calls=%async_computation.1 | async-start | bytes 262144 | tf_op jit(solution)/shard_map/all_to_all | solution.py:141
  444.0 14.9 %all-to-all-done.1 = f32[64,1,416]{2,1,0:T(1,128)S(1)} async-done(((f32[64,1,416]{2,1,0:T(1,128)}), f32[64,1,416]{2,1,0:T(1,128)S(1)}, u32[]{:S(2)}, u32[]{:S(2)}) %all-to-all-start.1) | async-done | bytes 106528 | tf_op jit(solution)/shard_map/all_to_all | solution.py:141
  459.9 11.8 %reshape.316 = f32[3328,2,2,2]{3,2,1,0:T(2,128)} reshape(f32[64,416]{1,0:T(8,128)S(1)} %reduce.2) | data formatting | bytes 212992
  471.7 10.3 %copy.165 = f32[2,2,2,64,52]{4,3,2,1,0:T(8,128)S(1)} copy(f32[2,2,2,64,52]{2,1,0,4,3:T(2,128)} %bitcast.226) | data formatting | bytes 212992 | tf_op jit(solution)/shard_map/all_to_all | solution.py:141
  482.9 140.8 %psum.15 = f32[2]{0:T(128)S(1)} all-reduce(f32[2]{0:T(128)S(1)} %broadcast_multiply_fusion.3), channel_id=1, replica_groups=mesh['band'=8,'pw'=64] {'pw'}, use_global_device_ids=true, to_apply=%region_5.6 | all-reduce | flops 2 | bytes 16 | tf_op jit(solution)/shard_map/psum | solution.py:153
  626.7 22.6 %all_to_all.48 = f32[64,1,832]{2,1,0:T(1,128)S(1)} all-to-all(f32[64,1,832]{2,1,0:T(1,128)S(1)} %reshape.317), channel_id=1, replica_groups=mesh['band'=8,'pw'=64] {'pw'}, dimensions={0} | all-to-all | bytes 425984 | tf_op jit(solution)/shard_map/all_to_all | solution.py:59
  652.5 60.0 %gather_fusion.2 = f32[16384,16]{1,0:T(8,128)} fusion(f32[3329,16]{1,0:T(8,128)S(1)} %concatenate.11, s32[16384]{0:T(1024)} %fusion.49), kind=kCustom, calls=%fused_computation.2 | custom fusion | bytes 2162688 | tf_op jit(solution)/shard_map/jit(_take)/gather | solution.py:67
  712.4 13.2 %select_bitcast_fusion = f32[16,16384]{0,1:T(8,128)} fusion(f32[16384,16]{1,0:T(8,128)} %gather_fusion.2, pred[16384]{0:T(1024)(128)(4,1)S(1)} %copy-done.25), kind=kLoop, calls=%fused_computation.4 | loop fusion | flops 262144 | bytes 2113536 | tf_op jit(solution)/shard_map/jit(_take)/select_n | solution.py:67
  725.6 5.2 copy.118
  730.8 2.0 convolution_bitcast_fusion
  732.8 1.9 fusion.20
  737.5 27.2 %reduce-scatter.2.cloned.1.call-done = f32[2,16,128]{2,1,0:T(8,128)} async-done(((f32[2,128,128]{2,1,0:T(8,128)}), f32[2,16,128]{2,1,0:T(8,128)}) %reduce-scatter.2.cloned.1.call-update) | async-done | bytes 16400 | tf_op jit(solution)/shard_map/reduce_scatter | solution.py:163
  (147 shorter events, 41.1 us)
Async XLA Ops:
  7.2 303.2 %copy-start = (f32[16]{0:T(128)S(1)}, f32[16]{0:T(128)}, u32[]{:S(2)}) copy-start(f32[16]{0:T(128)} %param.16) | copy-start | bytes 196
  7.2 303.1 %copy-start.31 = (s32[16]{0:T(128)S(1)}, s32[16]{0:T(128)}, u32[]{:S(2)}) copy-start(s32[16]{0:T(128)} %param.17) | copy-start | bytes 196
  8.6 304.7 %copy-start.13 = (f32[52,128]{1,0:T(8,128)}, f32[52,128]{1,0:T(8,128)S(1)}, u32[]{:S(2)}) copy-start(f32[52,128]{1,0:T(8,128)S(1)} %fusion.58) | copy-start | bytes 79876
  158.8 155.3 %copy-start.6 = (f32[2,2,52,128]{3,2,1,0:T(8,128)}, f32[2,2,52,128]{3,2,1,0:T(8,128)S(1)}, u32[]{:S(2)}) copy-start(f32[2,2,52,128]{3,2,1,0:T(8,128)S(1)} %multiply_add_fusion) | copy-start | bytes 319492
  162.0 149.3 %all-to-all-start = ((f32[64,1,416]{2,1,0:T(1,128)}), f32[64,1,416]{2,1,0:T(1,128)S(1)}, u32[]{:S(2)}, u32[]{:S(2)}) async-start(f32[64,1,416]{2,1,0:T(1,128)} %reshape.313), calls=%async_computation | async-start | bytes 262144 | tf_op jit(solution)/shard_map/all_to_all | solution.py:59
  314.2 60.5 %copy-start.24 = (pred[16384]{0:T(1024)(128)(4,1)S(1)}, pred[16384]{0:T(1024)(128)(4,1)}, u32[]{:S(2)}) copy-start(pred[16384]{0:T(1024)(128)(4,1)} %compare_and_fusion) | copy-start | bytes 49156
  414.1 29.9 %copy-start.20 = (f32[2,52,128]{2,0,1:T(2,128)S(1)}, f32[2,52,128]{2,0,1:T(2,128)}, u32[]{:S(2)}) copy-start(f32[2,52,128]{2,0,1:T(2,128)} %fusion.15) | copy-start | bytes 159748
  414.1 29.9 %copy-start.21 = (f32[2,52,128]{2,0,1:T(2,128)S(1)}, f32[2,52,128]{2,0,1:T(2,128)}, u32[]{:S(2)}) copy-start(f32[2,52,128]{2,0,1:T(2,128)} %fusion.17) | copy-start | bytes 159748
  414.1 29.9 %copy-start.22 = (f32[2,52,128]{2,0,1:T(2,128)S(1)}, f32[2,52,128]{2,0,1:T(2,128)}, u32[]{:S(2)}) copy-start(f32[2,52,128]{2,0,1:T(2,128)} %fusion.14) | copy-start | bytes 159748
  414.1 29.9 %copy-start.23 = (f32[2,52,128]{2,0,1:T(2,128)S(1)}, f32[2,52,128]{2,0,1:T(2,128)}, u32[]{:S(2)}) copy-start(f32[2,52,128]{2,0,1:T(2,128)} %fusion.16) | copy-start | bytes 159748
  430.8 51.4 %copy-start.7 = (f32[2,2,52,128]{3,2,1,0:T(8,128)S(1)}, f32[2,2,52,128]{3,2,1,0:T(8,128)}, u32[]{:S(2)}) copy-start(f32[2,2,52,128]{3,2,1,0:T(8,128)} %copy-done.6) | copy-start | bytes 319492
  430.8 51.4 %copy-start.10 = (f32[1,2,128,128]{3,2,1,0:T(8,128)S(1)}, f32[1,2,128,128]{3,2,1,0:T(8,128)}, u32[]{:S(2)}) copy-start(f32[1,2,128,128]{3,2,1,0:T(8,128)} %get-tuple-element.22) | copy-start | bytes 393220
  430.8 51.4 %copy-start.12 = (f32[1,2,128,128]{3,2,1,0:T(8,128)S(1)}, f32[1,2,128,128]{3,2,1,0:T(8,128)}, u32[]{:S(2)}) copy-start(f32[1,2,128,128]{3,2,1,0:T(8,128)} %get-tuple-element.25) | copy-start | bytes 393220
  430.8 51.4 %copy-start.27 = (f32[52,128]{1,0:T(8,128)S(1)}, f32[52,128]{1,0:T(8,128)}, u32[]{:S(2)}) copy-start(f32[52,128]{1,0:T(8,128)} %get-tuple-element.30) | copy-start | bytes 79876
  430.8 192.9 %copy-start.33 = (f32[2]{0:T(128)S(1)}, f32[2]{0:T(128)}, u32[]{:S(2)}) copy-start(f32[2]{0:T(128)} %copy-done.32) | copy-start | bytes 28
  430.8 192.9 %copy-start.14 = (f32[52,128]{1,0:T(8,128)S(1)}, f32[52,128]{1,0:T(8,128)}, u32[]{:S(2)}) copy-start(f32[52,128]{1,0:T(8,128)} %copy-done.13) | copy-start | bytes 79876
  430.8 192.9 %copy-start.17 = (f32[2,2,52,128]{3,1,2,0:T(2,128)S(1)}, f32[2,2,52,128]{3,1,2,0:T(2,128)}, u32[]{:S(2)}) copy-start(f32[2,2,52,128]{3,1,2,0:T(2,128)} %param.12) | copy-start | bytes 319492
  430.9 192.9 %copy-start.29 = (f32[2,2,52,128]{3,1,2,0:T(2,128)S(1)}, f32[2,2,52,128]{3,1,2,0:T(2,128)}, u32[]{:S(2)}) copy-start(f32[2,2,52,128]{3,1,2,0:T(2,128)} %param.11) | copy-start | bytes 319492
  430.9 28.1 %all-to-all-start.1 = ((f32[64,1,416]{2,1,0:T(1,128)}), f32[64,1,416]{2,1,0:T(1,128)S(1)}, u32[]{:S(2)}, u32[]{:S(2)}) async-start(f32[64,1,416]{2,1,0:T(1,128)} %reshape.315), calls=%async_computation.1 | async-start | bytes 262144 | tf_op jit(solution)/shard_map/all_to_all | solution.py:141
  443.8 320.9 %reduce-scatter.2.cloned.1.call-start = ((), (), s32[]{:S(2)}) async-start(), calls=%async_computation.4 | async-start | bytes 147456 | tf_op jit(solution)/shard_map/reduce_scatter | solution.py:163
  444.0 181.1 %copy-start.4 = (f32[1,2,128,128]{3,2,0,1:T(8,128)S(1)}, f32[1,2,128,128]{3,2,0,1:T(8,128)}, u32[]{:S(2)}) copy-start(f32[1,2,128,128]{3,2,0,1:T(8,128)} %copy-done.2) | copy-start | bytes 393220
  444.0 181.1 %copy-start.19 = (f32[2,2,52,128]{3,2,1,0:T(8,128)S(1)}, f32[2,2,52,128]{3,2,1,0:T(8,128)}, u32[]{:S(2)}) copy-start(f32[2,2,52,128]{3,2,1,0:T(8,128)} %get-tuple-element.28) | copy-start | bytes 319492
  652.4 60.0 %copy-start.25 = (pred[16384]{0:T(1024)(128)(4,1)S(1)}, pred[16384]{0:T(1024)(128)(4,1)}, u32[]{:S(2)}) copy-start(pred[16384]{0:T(1024)(128)(4,1)} %compare_and_fusion) | copy-start | bytes 49156
  712.4 52.3 %copy-start.1 = (f32[16]{0:T(128)S(1)}, f32[16]{0:T(128)}, u32[]{:S(2)}) copy-start(f32[16]{0:T(128)} %param.16) | copy-start | bytes 196
  (13 other events, 111.4 us)
Sparse Core Ops, SparseCore 0:
  735.5 29.1 reduce-scatter.1
